TPU v7x, 128 devices: a whole 4x4x4 slice. The times are simulated.
128 devices in a mesh: plane: 64 (over x, y, z), cuts: 2 (over core).
Axes of the slice: x: 4, y: 4, z: 4, core: 2. Of those that a mesh axis runs over, the one named last changes fastest.
Arguments:
- image: float32 [1024, 128, 256], P('plane', None, 'cuts'), may hold values from 0 to 2
- projection_weight_tiles: bfloat16 [6144, 256, 256], P('plane'), may hold values from -0.0390625 to 0.0390625
- pair_tile_index: int32 [6144], P('plane'), may hold values from 0 to 7
- pair_ray_block: int32 [6144], P('plane'), may hold values from 0 to 63
- ray_owner: int32 [64], replicated, may hold values from 0 to 63, each once
- active_pair_count: int32 [64], P('plane'), may hold values from 12 to 96, as said below
- measured: float32 [64, 256, 256], P('plane', None, 'cuts'), may hold values from -6 to 6
Outputs:
- volume: float32 [1024, 128, 256], P('plane', None, 'cuts')
- residual: bfloat16 [64, 256, 256], P('plane', None, 'cuts')
Inputs may be any that keep to these rules, and one draw needn't show every extreme that they name: The first active_pair_count[d] pairs of plane index d are live and the rest are not; some index has all 96 pairs live. `ray_owner`: each owner position is taken by exactly one ray block.
All inputs are finite; a program needn't handle non-finite values.
Results may differ from a plain program's by a relative error of at most 0.0045.
Values may be sent and summed in bfloat16 or wider, within the bound.
A program may use at most 128 MiB of HBM per device.

v0:
```python
import jax
import jax.numpy as jnp
from jax import lax
from jax.sharding import PartitionSpec as P

TILE = 16
SWEEPS = 4


smooth_square = 0.09
flow_step = 0.04
relax_step = 4.0
group_width = 32


def with_halo(block, sides, width):
    for axis, dim in sides:
        count = lax.axis_size(axis)
        forward = [(i, i + 1) for i in range(count - 1)]
        backward = [(target, source) for source, target in forward]
        low = lax.ppermute(
            lax.slice_in_dim(block, block.shape[dim] - width, None, axis=dim), axis, forward
        )
        high = lax.ppermute(lax.slice_in_dim(block, 0, width, axis=dim), axis, backward)
        block = jnp.concatenate([low, block, high], axis=dim)
    return block


def smooth_sweep(volume, inside):
    rise_rows = jnp.concatenate([volume[1:] - volume[:-1], -volume[-1:]], axis=0)
    rise_cols = jnp.concatenate([volume[:, 1:] - volume[:, :-1], -volume[:, -1:]], axis=1)
    rise_slices = jnp.concatenate(
        [volume[:, :, 1:] - volume[:, :, :-1], -volume[:, :, -1:]], axis=2
    )
    length = jnp.sqrt(
        smooth_square + rise_rows * rise_rows + rise_cols * rise_cols + rise_slices * rise_slices
    )
    flow_rows = rise_rows / length * inside
    flow_cols = rise_cols / length * inside
    flow_slices = rise_slices / length * inside
    diverge = flow_rows - jnp.concatenate([jnp.zeros_like(flow_rows[:1]), flow_rows[:-1]], axis=0)
    diverge = (
        diverge
        + flow_cols
        - jnp.concatenate([jnp.zeros_like(flow_cols[:, :1]), flow_cols[:, :-1]], axis=1)
    )
    diverge = (
        diverge
        + flow_slices
        - jnp.concatenate([jnp.zeros_like(flow_slices[:, :, :1]), flow_slices[:, :, :-1]], axis=2)
    )
    return (volume + flow_step * diverge) * inside


def per_device(
    image,
    projection_weight_tiles,
    pair_tile_index,
    pair_ray_block,
    ray_owner,
    active_pair_count,
    measured,
):
    row_count, col_count, slice_count = image.shape
    slot_total, voxels, ray_count = projection_weight_tiles.shape
    tile_rows = row_count // TILE
    tile_cols = col_count // TILE
    tiles_here = tile_rows * tile_cols
    block_count = slot_total // group_width
    ray_blocks = ray_owner.shape[0]
    grouped = (
        image.reshape(tile_rows, TILE, tile_cols, TILE, slice_count)
        .transpose(0, 2, 1, 3, 4)
        .reshape(tiles_here, voxels, slice_count)
        .astype(jnp.bfloat16)
    )
    owner_of = ray_owner[pair_ray_block]
    active_pair = jnp.arange(slot_total, dtype=jnp.int32) < active_pair_count[0]

    def block_parts(block_index):
        first_slot = block_index * group_width
        weights = lax.dynamic_slice_in_dim(projection_weight_tiles, first_slot, group_width, 0)
        tile_ids = lax.dynamic_slice_in_dim(pair_tile_index, first_slot, group_width, 0)
        owners = lax.dynamic_slice_in_dim(owner_of, first_slot, group_width, 0)
        live_part = lax.dynamic_slice_in_dim(active_pair, first_slot, group_width, 0)
        return (weights, tile_ids, owners, live_part)

    def forward(block_index, running):
        weights, tile_ids, owners, live_part = block_parts(block_index)
        values = jnp.take(grouped, tile_ids, axis=0)
        product = jnp.einsum("svr,svc->src", weights, values, preferred_element_type=jnp.float32)
        product = jnp.where(live_part[:, None, None], product, 0.0)
        return running.at[owners].add(product)

    partials = lax.fori_loop(
        0, block_count, forward, jnp.zeros((ray_blocks, ray_count, slice_count), jnp.float32)
    )
    own_sums = lax.psum_scatter(partials, "plane", scatter_dimension=0, tiled=True)
    mismatch = measured - own_sums
    residual = (mismatch / jnp.sqrt(1.0 + mismatch * mismatch)).astype(jnp.bfloat16)
    spread = lax.all_gather(residual, "plane", axis=0, tiled=True)

    def backward(block_index, running):
        weights, tile_ids, owners, live_part = block_parts(block_index)
        values = jnp.take(spread, owners, axis=0)
        product = jnp.einsum("svr,src->svc", weights, values, preferred_element_type=jnp.float32)
        product = jnp.where(live_part[:, None, None], product, 0.0)
        return running.at[tile_ids].add(product)

    update = lax.fori_loop(
        0, block_count, backward, jnp.zeros((tiles_here, voxels, slice_count), jnp.float32)
    )
    update = (
        update.reshape(tile_rows, tile_cols, TILE, TILE, slice_count)
        .transpose(0, 2, 1, 3, 4)
        .reshape(row_count, col_count, slice_count)
    )
    volume = jnp.maximum(image + relax_step * update, 0.0)
    row_start = lax.axis_index("plane") * row_count - 1
    slice_start = lax.axis_index("cuts") * slice_count - 1
    row_ids = row_start + jnp.arange(row_count + 2 * 1, dtype=jnp.int32)
    slice_ids = slice_start + jnp.arange(slice_count + 2 * 1, dtype=jnp.int32)
    row_inside = (row_ids >= 0) & (row_ids < row_count * lax.axis_size("plane"))
    slice_inside = (slice_ids >= 0) & (slice_ids < slice_count * lax.axis_size("cuts"))
    inside = (row_inside[:, None, None] & slice_inside[None, None, :]).astype(jnp.float32)
    for repeat in range(SWEEPS):
        padded = with_halo(volume, (("plane", 0), ("cuts", 2)), 1)
        volume = smooth_sweep(padded, inside)[1:-1, :, 1:-1]
    return (volume, residual)


def solution(mesh):
    placed = (
        P("plane", None, "cuts"),
        P("plane", None, None),
        P("plane"),
        P("plane"),
        P(),
        P("plane"),
        P("plane", None, "cuts"),
    )
    return jax.shard_map(
        per_device,
        mesh=mesh,
        in_specs=placed,
        out_specs=(P("plane", None, "cuts"), P("plane", None, "cuts")),
        check_vma=False,
    )
```

profile of v0, /device:TPU:121, one launch (start us, length us, event | category | flops | bytes accessed | tf_op | source)
XLA Modules:
  0.0 707.8 jit_solution(18205141428263837241)
XLA Ops:
  11.2 4.3 broadcast_in_dim.125
  15.5 51.1 %while.26 = (s32[]{:T(128)}, f32[64,256,128]{2,1,0:T(8,128)}, s32[96]{0:T(128)S(1)}, pred[96]{0:T(512)(128)(4,1)S(1)}, bf16[96,256,256]{2,1,0:T(8,128)(2,1)}, /*...) while((s32[]{:T(128)}, f32[64,256,128]{2,1,0:T(8,128)}, ...), condition=%wide.region_2.3_spmd, body=%wide.region_0.2_spmd.sunk | while | flops 540017984 | bytes 27268300 | solution.py:95
  16.6 5.9 fusion.38
  22.6 9.9 %scatter_fusion = f32[64,256,128]{2,1,0:T(8,128)} fusion(f32[64,256,128]{2,1,0:T(8,128)} %get-tuple-element.462, s32[32]{0:T(128)S(1)} %compare_select_fusion.9, f32[32,256,128]{2,1,0:T(8,128)} %fusion.38), kind=kCustom, calls=%fused_computation.3.clone.1 | custom fusion | flops 1048576 | bytes 12583040 | tf_op jit(solution)/shard_map/while/body/eval_jaxpr/scatter-add | solution.py:93
  33.7 5.9 fusion.38
  39.6 10.0 %scatter_fusion = f32[64,256,128]{2,1,0:T(8,128)} fusion(f32[64,256,128]{2,1,0:T(8,128)} %get-tuple-element.462, s32[32]{0:T(128)S(1)} %compare_select_fusion.9, f32[32,256,128]{2,1,0:T(8,128)} %fusion.38), kind=kCustom, calls=%fused_computation.3.clone.1 | custom fusion | flops 1048576 | bytes 12583040 | tf_op jit(solution)/shard_map/while/body/eval_jaxpr/scatter-add | solution.py:93
  50.8 5.9 fusion.38
  56.7 9.8 %scatter_fusion = f32[64,256,128]{2,1,0:T(8,128)} fusion(f32[64,256,128]{2,1,0:T(8,128)} %get-tuple-element.462, s32[32]{0:T(128)S(1)} %compare_select_fusion.9, f32[32,256,128]{2,1,0:T(8,128)} %fusion.38), kind=kCustom, calls=%fused_computation.3.clone.1 | custom fusion | flops 1048576 | bytes 12583040 | tf_op jit(solution)/shard_map/while/body/eval_jaxpr/scatter-add | solution.py:93
  66.7 283.9 %reduce-scatter.2.cloned.1.call-done = f32[1,256,128]{2,1,0:T(8,128)} async-done(((f32[64,256,128]{2,1,0:T(8,128)}), f32[1,256,128]{2,1,0:T(8,128)}) %reduce-scatter.2.cloned.1.call-update) | async-done | bytes 131088 | tf_op jit(solution)/shard_map/reduce_scatter | solution.py:98
  352.2 150.1 %all-gather.2.cloned.1.call-done = bf16[64,256,128]{2,1,0:T(8,128)(2,1)} async-done(((bf16[1,256,128]{2,1,0:T(8,128)(2,1)}), bf16[64,256,128]{2,1,0:T(8,128)(2,1)}) %all-gather.2.cloned.1.call-update) | async-done | bytes 4194320 | tf_op jit(solution)/shard_map/all_gather | solution.py:101
  502.4 46.1 %while.27 = (s32[]{:T(128)}, f32[8,256,128]{2,1,0:T(8,128)S(1)}, s32[96]{0:T(128)S(1)}, pred[96]{0:T(512)(128)(4,1)S(1)}, bf16[96,256,256]{2,1,0:T(8,128)(2,1)},...) while((s32[]{:T(128)}, f32[8,256,128]{2,1,0:T(8,128)S(1)}, ...), condition=%wide.region_6.7_spmd, body=%wide.region_4.6_spmd.sunk | while | flops 540017984 | bytes 27268300 | solution.py:110
  502.5 3.1 gather_fusion.1
  505.7 5.5 fusion.41
  511.3 6.4 scatter_fusion.1
  517.9 3.1 gather_fusion.1
  521.1 5.5 fusion.41
  526.7 6.5 scatter_fusion.1
  533.3 3.1 gather_fusion.1
  536.5 5.5 fusion.41
  542.1 6.4 scatter_fusion.1
  549.9 4.5 collective-permute-start
  556.3 7.3 %collective-permute-done.1 = f32[1,128,128]{2,1,0:T(8,128)S(1)} collective-permute-done((f32[1,128,128]{2,1,0:T(8,128)S(1)}, f32[1,128,128]{2,1,0:T(8,128)S(1)}, u32[]{:S(2)}, u32[]{:S(2)}) %collective-permute-start.1) | collective-permute-done | bytes 65568 | tf_op jit(solution)/shard_map/ppermute | solution.py:24
  565.2 4.9 collective-permute-start.3
  592.2 3.4 collective-permute-start.5
  595.9 5.9 collective-permute-done.5
  605.2 3.6 collective-permute-start.7
  627.7 3.4 collective-permute-start.9
  631.4 5.8 collective-permute-done.9
  640.6 3.2 collective-permute-start.11
  662.9 3.4 collective-permute-start.13
  666.6 5.5 collective-permute-done.13
  675.5 3.6 collective-permute-start.15
  (198 shorter events, 106.5 us)
Async XLA Ops:
  7.2 2.8 copy-start
  7.2 343.4 %reduce-scatter.2.cloned.1.call-start = ((), (), s32[]{:S(2)}) async-start(), calls=%async_computation.1 | async-start | bytes 8519680 | tf_op jit(solution)/shard_map/reduce_scatter | solution.py:98
  11.2 4.3 copy-start.27
  66.6 284.0 %copy-start.26 = (f32[1,256,128]{2,1,0:T(8,128)S(1)}, f32[1,256,128]{2,1,0:T(8,128)}, u32[]{:S(2)}) copy-start(f32[1,256,128]{2,1,0:T(8,128)} %param.17) | copy-start | bytes 393220
  66.6 435.7 %all-gather.2.cloned.1.call-start = ((), (), s32[]{:S(2)}) async-start(), calls=%async_computation.2 | async-start | bytes 4259840 | tf_op jit(solution)/shard_map/all_gather | solution.py:101
  549.9 6.4 collective-permute-start
  554.4 9.2 %collective-permute-start.1 = (f32[1,128,128]{2,1,0:T(8,128)S(1)}, f32[1,128,128]{2,1,0:T(8,128)S(1)}, u32[]{:S(2)}, u32[]{:S(2)}) collective-permute-start(f32[1,128,128]{2,1,0:T(8,128)S(1)} %get-tuple-element.355), channel_id=1, source_target_pairs={{2,0},{4,2},{6,4},{8,6},{10,8},{12,10},{14,12},{16,14},{18,16},{20... | collective-permute-start | bytes 196616 | tf_op jit(solution)/shard_map/ppermute | solution.py:24
  565.2 7.1 collective-permute-start.3
  570.6 3.1 collective-permute-start.2
  581.4 2.4 copy-start.8
  581.4 2.7 copy-start.11
  581.4 2.7 copy-start.23
  590.3 5.6 collective-permute-start.4
  592.2 9.6 %collective-permute-start.5 = (f32[1,128,128]{2,1,0:T(8,128)S(1)}, f32[1,128,128]{2,1,0:T(8,128)S(1)}, u32[]{:S(2)}, u32[]{:S(2)}) collective-permute-start(f32[1,128,128]{2,1,0:T(8,128)S(1)} %get-tuple-element.345), channel_id=1, source_target_pairs={{2,0},{4,2},{6,4},{8,6},{10,8},{12,10},{14,12},{16,14},{18,16},{20... | collective-permute-start | bytes 196616 | tf_op jit(solution)/shard_map/ppermute | solution.py:24
  603.4 5.3 collective-permute-start.6
  605.2 4.0 collective-permute-start.7
  616.8 2.7 copy-start.12
  616.8 2.7 copy-start.24
  625.7 5.6 collective-permute-start.8
  627.7 9.6 %collective-permute-start.9 = (f32[1,128,128]{2,1,0:T(8,128)S(1)}, f32[1,128,128]{2,1,0:T(8,128)S(1)}, u32[]{:S(2)}, u32[]{:S(2)}) collective-permute-start(f32[1,128,128]{2,1,0:T(8,128)S(1)} %get-tuple-element.343), channel_id=1, source_target_pairs={{2,0},{4,2},{6,4},{8,6},{10,8},{12,10},{14,12},{16,14},{18,16},{20... | collective-permute-start | bytes 196616 | tf_op jit(solution)/shard_map/ppermute | solution.py:24
  638.8 5.0 collective-permute-start.10
  640.6 3.9 collective-permute-start.11
  652.1 2.7 copy-start.13
  652.1 2.7 copy-start.25
  661.0 5.6 collective-permute-start.12
  662.9 9.2 %collective-permute-start.13 = (f32[1,128,128]{2,1,0:T(8,128)S(1)}, f32[1,128,128]{2,1,0:T(8,128)S(1)}, u32[]{:S(2)}, u32[]{:S(2)}) collective-permute-start(f32[1,128,128]{2,1,0:T(8,128)S(1)} %get-tuple-element.341), channel_id=1, source_target_pairs={{2,0},{4,2},{6,4},{8,6},{10,8},{12,10},{14,12},{16,14},{18,16},{20... | collective-permute-start | bytes 196616 | tf_op jit(solution)/shard_map/ppermute | solution.py:24
  673.8 5.5 collective-permute-start.14
  675.5 5.1 collective-permute-start.15
  690.6 2.6 copy-start.2
  690.6 3.1 copy-start.3
  690.6 3.4 copy-start.4
  690.6 3.4 copy-start.15
  (14 other events, 18.5 us)
Sparse Core Ops, SparseCore 0:
  66.7 283.8 reduce-scatter.1
  354.0 148.2 all-gather.1
where the time goes:
time: 716 us; the launch traced here: 708 us
  waiting for transfers between devices  460 us (64%)
  other arithmetic  109 us (15%)
  local copies, waits for them, and re-layouts  46.4 us (6%)
  starting transfers between devices  43.1 us (6%)
  matrix products  34.2 us (5%)
  between operations  15.6 us (2%)
    reduce_scatter x1, waiting for transfers between devices, per_device(): lax.psum_scatter(partials, 'plane', scatter_dimension=0, tiled=True)  284 us
    all_gather x1, waiting for transfers between devices, per_device(): spread = lax.all_gather(residual, 'plane', axis=0, tiled=True)  150 us
    scatter-add x3, other arithmetic, forward(): return running.at[owners].add(product)  29.8 us
    ppermute x8, starting transfers between devices, with_halo(): lax.ppermute(lax.slice_in_dim(block, 0, width, axis=dim), axis, backward)  27.3 us
    ppermute x8, waiting for transfers between devices, with_halo(): lax.ppermute(lax.slice_in_dim(block, 0, width, axis=dim), axis, backward)  24.8 us
    scatter-add x3, other arithmetic, backward(): return running.at[tile_ids].add(product)  19.4 us
    dot_general x3, matrix products, forward(): jnp.einsum('svr,svc->src', weights, values, preferred_element_type=jnp.fl...  17.6 us
    dot_general x3, matrix products, backward(): jnp.einsum('svr,src->svc', weights, values, preferred_element_type=jnp.fl...  16.5 us
  transfers between devices with their start and end apart: 18, of which 8 were waited for; matrix products, arithmetic and copies ran while one was open for 1% of the time, Pallas kernels for 0%

commit v1 on v0

v1 whole, which is shorter than its diff:
```python
import functools

import jax
import jax.numpy as jnp
from jax import lax
from jax.experimental import pallas as pl
from jax.experimental.pallas import tpu as pltpu
from jax.sharding import PartitionSpec as P

TILE = 16
SWEEPS = 4
smooth_square = 0.09
flow_step = 0.04
relax_step = 4.0

SIDE = 4
GROUP = 8
HALO = 4
VMEM_LIMIT = 60 * 1024 * 1024
ORDERS = ((0, 1, 2), (1, 2, 0), (2, 0, 1))
SUM_ROWS = ((0, 48), (48, 48), (96, 32))
SPREAD_ROWS = ((0, 96), (96, 80), (176, 80))

F32 = jnp.float32
BF16 = jnp.bfloat16


def coordinates():
    here = lax.axis_index("plane")
    return here // (SIDE * SIDE), (here // SIDE) % SIDE, here % SIDE


def relative_slot(owner):
    x, y, z = coordinates()
    dx = lax.bitwise_and(owner // (SIDE * SIDE) - x + SIDE, SIDE - 1)
    dy = lax.bitwise_and((owner // SIDE) % SIDE - y + SIDE, SIDE - 1)
    dz = lax.bitwise_and(owner % SIDE - z + SIDE, SIDE - 1)
    return (dx * SIDE + dy) * SIDE + dz


def forward_kernel(tiles, blocks, owners, count, image, weights, out, voxels, sums):
    step = pl.program_id(0)
    slots = sums.shape[0] - 1

    @pl.when(step == 0)
    def _():
        for tile in range(voxels.shape[0]):
            piece = image[:, tile * TILE : (tile + 1) * TILE, :]
            voxels[tile] = piece.reshape(TILE * TILE, piece.shape[-1]).T.astype(BF16)

        def clear(i, c):
            sums[i] = jnp.zeros(sums.shape[1:], F32)
            return c

        lax.fori_loop(0, slots, clear, 0)

    for i in range(GROUP):
        pair = step * GROUP + i
        slot = jnp.where(pair < count[0], relative_slot(owners[blocks[pair]]), slots)
        product = jnp.dot(voxels[tiles[pair]], weights[i], preferred_element_type=F32)
        sums[slot, 0] += product[:, :128]
        sums[slot, 1] += product[:, 128:]

    @pl.when(step == pl.num_programs(0) - 1)
    def _():
        def finish(i, c):
            out[i] = sums[i].astype(BF16)
            return c

        lax.fori_loop(0, slots, finish, 0)


def forward(tiles, blocks, owners, count, image, weights):
    pairs, voxels, rays = weights.shape
    rows, cols, slices = image.shape
    slots = owners.shape[0]
    tile_count = cols // TILE
    return pl.pallas_call(
        forward_kernel,
        out_shape=jax.ShapeDtypeStruct((slots, 2, slices, 128), BF16),
        grid_spec=pltpu.PrefetchScalarGridSpec(
            num_scalar_prefetch=4,
            grid=(pairs // GROUP,),
            in_specs=[
                pl.BlockSpec((rows, cols, slices), lambda i, *_: (0, 0, 0)),
                pl.BlockSpec((GROUP, voxels, rays), lambda i, *_: (i, 0, 0)),
            ],
            out_specs=pl.BlockSpec((slots, 2, slices, 128), lambda i, *_: (0, 0, 0, 0)),
            scratch_shapes=[
                pltpu.VMEM((tile_count, slices, voxels), BF16),
                pltpu.VMEM((slots + 1, 2, slices, 128), F32),
            ],
        ),
        compiler_params=pltpu.CompilerParams(vmem_limit_bytes=VMEM_LIMIT),
        name="project",
    )(tiles, blocks, owners, count, image, weights)


def backward_kernel(tiles, blocks, owners, count, image, spread, weights, out, sums):
    step = pl.program_id(0)
    tile_count = sums.shape[0] - 1

    @pl.when(step == 0)
    def _():
        for i in range(tile_count):
            sums[i] = jnp.zeros(sums.shape[1:], F32)

    for i in range(GROUP):
        pair = step * GROUP + i
        tile = jnp.where(pair < count[0], tiles[pair], tile_count)
        slot = relative_slot(owners[blocks[pair]])
        sums[tile] += jnp.dot(weights[i], spread[slot], preferred_element_type=F32)

    @pl.when(step == pl.num_programs(0) - 1)
    def _():
        def finish(row, c):
            start = pl.multiple_of(row * TILE, TILE)
            update = jnp.concatenate(
                [sums[tile, pl.ds(start, TILE), :] for tile in range(tile_count)], axis=0
            )
            out[row] = jnp.maximum(image[row] + relax_step * update, 0.0).T
            return c

        lax.fori_loop(0, image.shape[0], finish, 0)


def backward(tiles, blocks, owners, count, image, spread, weights):
    pairs, voxels, rays = weights.shape
    rows, cols, slices = image.shape
    slots = owners.shape[0]
    return pl.pallas_call(
        backward_kernel,
        out_shape=jax.ShapeDtypeStruct((rows, slices, cols), F32),
        grid_spec=pltpu.PrefetchScalarGridSpec(
            num_scalar_prefetch=4,
            grid=(pairs // GROUP,),
            in_specs=[
                pl.BlockSpec((rows, cols, slices), lambda i, *_: (0, 0, 0)),
                pl.BlockSpec((slots, rays, slices), lambda i, *_: (0, 0, 0)),
                pl.BlockSpec((GROUP, voxels, rays), lambda i, *_: (i, 0, 0)),
            ],
            out_specs=pl.BlockSpec((rows, slices, cols), lambda i, *_: (0, 0, 0)),
            scratch_shapes=[pltpu.VMEM((cols // TILE + 1, voxels, slices), F32)],
        ),
        compiler_params=pltpu.CompilerParams(vmem_limit_bytes=VMEM_LIMIT),
        name="backproject",
    )(tiles, blocks, owners, count, image, spread, weights)


def neighbour(dim, shift):
    place = list(coordinates())
    place[dim] = (place[dim] + shift + SIDE) % SIDE
    return (place[0] * SIDE + place[1]) * SIDE + place[2]


def pick(order, *where):
    index = [slice(None)] * 3
    for position, value in enumerate(where):
        index[ORDERS[order][position]] = value
    return tuple(index)


def exchange_kernel(
    partial, measured, residual, spread_out, part, total, own, gather, *rest
):
    opposite = [rest[3 * o : 3 * o + 3] for o in range(3)]
    direct = [rest[9 + 3 * o : 12 + 3 * o] for o in range(3)]
    sum_send, sum_recv, spread_send, spread_recv, local = rest[18:]

    barrier = pltpu.get_barrier_semaphore()
    for dim in range(3):
        for shift in (1, -1):
            pl.semaphore_signal(barrier, inc=1, device_id={"plane": neighbour(dim, shift)})
    load = pltpu.make_async_copy(partial, part, local.at[0])
    load.start()
    load.wait()
    pl.semaphore_wait(barrier, 6)

    def source(order, phase, j, half):
        first, rows = SUM_ROWS[order]
        if phase == 2:
            return total[order].at[j, half]
        return part.at[pick(order, *([0] * phase), j) + (half, pl.ds(first, rows))]

    def send_sum(order, phase, slot, src, dst, shift):
        number = (order * 3 + phase) * 6 + slot
        copy = pltpu.make_async_remote_copy(
            src_ref=src,
            dst_ref=dst,
            send_sem=sum_send.at[number],
            recv_sem=sum_recv.at[number],
            device_id={"plane": neighbour(ORDERS[order][phase], shift)},
        )
        copy.start()
        return copy

    def combine(phase, target, first, *others):
        if phase == 0:

            def body(i, c):
                for k in range(SIDE):
                    value = first[i, k].astype(F32)
                    for other in others:
                        value = value + other[i, k].astype(F32)
                    target[i, k] = value.astype(target.dtype)
                return c

            lax.fori_loop(0, SIDE, body, 0)
        elif phase == 1:
            for k in range(SIDE):
                value = first[k].astype(F32)
                for other in others:
                    value = value + other[k].astype(F32)
                target[k] = value.astype(target.dtype)
        else:
            value = first[...]
            for other in others:
                value = value + other[...]
            target[...] = value

    sends = []
    for phase in range(3):
        early = {}
        for order in range(3):
            opp, dirs = opposite[order][phase], direct[order][phase]
            early[order] = [
                send_sum(order, phase, 0, source(order, phase, 2, 0), opp.at[0], 1),
                send_sum(order, phase, 1, source(order, phase, 2, 1), opp.at[1], -1),
                send_sum(order, phase, 2, source(order, phase, 1, 1), dirs.at[0, 1], 1),
                send_sum(order, phase, 3, source(order, phase, 3, 0), dirs.at[1, 0], -1),
            ]
        late = {}
        for order in range(3):
            opp, dirs = opposite[order][phase], direct[order][phase]
            early[order][0].wait_recv()
            here = source(order, phase, 1, 0)
            combine(phase, here, here, opp.at[0])
            a = send_sum(order, phase, 4, here, dirs.at[0, 0], 1)
            early[order][1].wait_recv()
            here = source(order, phase, 3, 1)
            combine(phase, here, here, opp.at[1])
            b = send_sum(order, phase, 5, here, dirs.at[1, 1], -1)
            late[order] = [a, b]
        for order in range(3):
            dirs = direct[order][phase]
            for copy in early[order][2:] + late[order]:
                copy.wait_recv()
            first, rows = SUM_ROWS[order]
            for half in range(2):
                here = source(order, phase, 0, half)
                if phase == 0:
                    target = here
                elif phase == 1:
                    target = total[order].at[:, half]
                else:
                    target = own.at[half, pl.ds(first, rows)]
                combine(phase, target, here, dirs.at[0, half], dirs.at[1, half])
            sends += early[order] + late[order]

    for half in range(2):
        rows = pl.ds(half * 128, 128)
        mismatch = measured[0, rows, :] - own[half].T
        value = (mismatch * lax.rsqrt(1.0 + mismatch * mismatch)).astype(BF16)
        residual[0, rows, :] = value
        gather[0, 0, 0, rows, :] = value

    def send_spread(order, phase, slot, src, dst, shift):
        number = (order * 3 + phase) * 4 + slot
        copy = pltpu.make_async_remote_copy(
            src_ref=src,
            dst_ref=dst,
            send_sem=spread_send.at[number],
            recv_sem=spread_recv.at[number],
            device_id={"plane": neighbour(ORDERS[order][phase], shift)},
        )
        copy.start()
        return copy

    def held(order, phase, j, first, rows):
        return gather.at[pick(order, *([0] * phase), j) + (pl.ds(first, rows),)]

    for phase in (2, 1, 0):
        early = {}
        for order in range(3):
            first, rows = SPREAD_ROWS[order]
            mine = held(order, phase, 0, first, rows)
            early[order] = [
                send_spread(order, phase, 0, mine, held(order, phase, 3, first, rows), 1),
                send_spread(order, phase, 1, mine, held(order, phase, 1, first, rows), -1),
            ]
        late = []
        for order in range(3):
            first, rows = SPREAD_ROWS[order]
            cut = 48
            early[order][0].wait_recv()
            a = send_spread(
                order, phase, 2, held(order, phase, 3, first, cut), held(order, phase, 2, first, cut), 1
            )
            early[order][1].wait_recv()
            first, rows = first + cut, rows - cut
            b = send_spread(
                order, phase, 3, held(order, phase, 1, first, rows), held(order, phase, 2, first, rows), -1
            )
            late += [a, b]
        for copy in late:
            copy.wait_recv()
        for order in range(3):
            sends += early[order]
        sends += late

    store = pltpu.make_async_copy(gather, spread_out, local.at[1])
    store.start()
    for copy in sends:
        copy.wait_send()
    store.wait()


def exchange(partial, measured):
    slots, halves, slices, lanes = partial.shape
    rays = measured.shape[1]
    cube = (SIDE, SIDE, SIDE)
    opposite, direct = [], []
    for order in range(3):
        rows = SUM_ROWS[order][1]
        for phase, (blocks, kind) in enumerate((((SIDE, SIDE), BF16), ((SIDE,), BF16), ((), F32))):
            opposite.append(pltpu.VMEM((2, *blocks, rows, lanes), kind))
            direct.append(pltpu.VMEM((2, 2, *blocks, rows, lanes), kind))

    def kernel(partial, measured, residual, spread_out, part, t0, t1, t2, own, gather, *rest):
        exchange_kernel(
            partial, measured, residual, spread_out, part, (t0, t1, t2), own, gather, *rest
        )

    residual, spread = pl.pallas_call(
        kernel,
        out_shape=(
            jax.ShapeDtypeStruct((1, rays, slices), BF16),
            jax.ShapeDtypeStruct((*cube, rays, slices), BF16),
        ),
        in_specs=[
            pl.BlockSpec(memory_space=pl.ANY),
            pl.BlockSpec(memory_space=pltpu.VMEM),
        ],
        out_specs=(pl.BlockSpec(memory_space=pltpu.VMEM), pl.BlockSpec(memory_space=pl.ANY)),
        scratch_shapes=[
            pltpu.VMEM((*cube, halves, slices, lanes), BF16),
            *[pltpu.VMEM((SIDE, halves, SUM_ROWS[o][1], lanes), F32) for o in range(3)],
            pltpu.VMEM((halves, slices, lanes), F32),
            pltpu.VMEM((*cube, rays, slices), BF16),
            *opposite,
            *direct,
            pltpu.SemaphoreType.DMA((54,)),
            pltpu.SemaphoreType.DMA((54,)),
            pltpu.SemaphoreType.DMA((36,)),
            pltpu.SemaphoreType.DMA((36,)),
            pltpu.SemaphoreType.DMA((2,)),
        ],
        compiler_params=pltpu.CompilerParams(
            collective_id=0, has_side_effects=True, vmem_limit_bytes=VMEM_LIMIT
        ),
        name="exchange",
    )(partial.reshape(*cube, halves, slices, lanes), measured)
    return residual, spread.reshape(slots, rays, slices)


def sweep_kernel(relaxed, out, field, other, flux_rows, flux_slices, edge, side, corner, *sems):
    row_send, row_recv, side_send, side_recv = sems
    rows, slices, cols = relaxed.shape
    here = lax.axis_index("plane")
    cut = lax.axis_index("cuts")
    last = lax.axis_size("plane") - 1
    up = (here + last) % (last + 1)
    down = (here + 1) % (last + 1)
    base = 8 + 8 * cut

    barrier = pltpu.get_barrier_semaphore()
    for plane in (up, down):
        for core in (0, 1):
            pl.semaphore_signal(barrier, inc=1, device_id={"plane": plane, "cuts": core})
    pl.semaphore_signal(barrier, inc=1, device_id={"plane": here, "cuts": 1 - cut})
    pl.semaphore_wait(barrier, 5)

    edge[0] = relaxed[rows - HALO :].astype(BF16)
    edge[1] = relaxed[:HALO].astype(BF16)
    start = pl.multiple_of(120 * (1 - cut), 8)
    side[0] = relaxed[:, pl.ds(start, 8), :]
    copies = []

    def send(src, dst, plane, core, number, which):
        copy = pltpu.make_async_remote_copy(
            src_ref=src,
            dst_ref=dst,
            send_sem=which[0].at[number],
            recv_sem=which[1].at[number],
            device_id={"plane": plane, "cuts": core},
        )
        copy.start()
        copies.append(copy)

    send(side.at[0], side.at[1], here, 1 - cut, 0, (side_send, side_recv))
    send(side.at[0, pl.ds(rows - HALO, HALO)], corner.at[0], down, 1 - cut, 1, (side_send, side_recv))
    send(side.at[0, pl.ds(0, HALO)], corner.at[1], up, 1 - cut, 2, (side_send, side_recv))
    send(edge.at[0], edge.at[2], down, cut, 0, (row_send, row_recv))
    send(edge.at[1], edge.at[3], up, cut, 1, (row_send, row_recv))

    total = rows + 2 * HALO
    zero = jnp.zeros((8, cols), F32)
    chunks = (slices + 8) // 8

    def clear(i, c):
        for array in (field, other):
            array[i, pl.ds(0, 8), :] = zero
            array[i, pl.ds(slices + 16, 8), :] = zero
        return c

    lax.fori_loop(0, total, clear, 0)
    flux_slices[pl.ds(0, 8), :] = zero
    own = pl.multiple_of(base, 8)
    beyond = pl.multiple_of(8 + slices * (1 - cut), 8)
    field[pl.ds(HALO, rows), pl.ds(own, slices), :] = relaxed[...]
    for copy in copies:
        copy.wait_recv()
    above = (here > 0).astype(F32)
    below = (here < last).astype(F32)
    field[pl.ds(HALO, rows), pl.ds(beyond, 8), :] = side[1]
    field[pl.ds(0, HALO), pl.ds(own, slices), :] = edge[2].astype(F32) * above
    field[pl.ds(0, HALO), pl.ds(beyond, 8), :] = corner[0] * above
    field[pl.ds(HALO + rows, HALO), pl.ds(own, slices), :] = edge[3].astype(F32) * below
    field[pl.ds(HALO + rows, HALO), pl.ds(beyond, 8), :] = corner[1] * below

    lane = lax.broadcasted_iota(jnp.int32, (8, cols), 1)
    not_last = lane < cols - 1
    not_first = lane > 0
    first_row = here * rows - HALO
    row_limit = (last + 1) * rows

    def sweep(old, new, low, high):
        def row_body(r, store):
            inside = jnp.logical_and(first_row + r >= 0, first_row + r < row_limit).astype(F32)
            for chunk in range(chunks):
                at = 8 + 8 * chunk
                value = old[r, at : at + 8, :]
                rise_rows = old[r + 1, at : at + 8, :] - value
                rise_slices = old[r, at + 1 : at + 9, :] - value
                rise_cols = jnp.where(not_last, pltpu.roll(value, cols - 1, 1), 0.0) - value
                square = rise_rows * rise_rows + rise_cols * rise_cols + rise_slices * rise_slices
                scale = lax.rsqrt(smooth_square + square) * inside
                along_rows = rise_rows * scale
                if store:
                    along_cols = rise_cols * scale
                    along_slices = rise_slices * scale
                    flux_slices[at : at + 8, :] = along_slices
                    diverge = along_rows - flux_rows[at : at + 8, :]
                    before = jnp.where(not_first, pltpu.roll(along_cols, 1, 1), 0.0)
                    diverge = diverge + (along_cols - before)
                    diverge = diverge + (along_slices - flux_slices[at - 1 : at + 7, :])
                    new[r, at : at + 8, :] = (value + flow_step * diverge) * inside
                flux_rows[at : at + 8, :] = along_rows

        row_body(low - 1, False)

        def body(r, c):
            row_body(r, True)
            return c

        lax.fori_loop(low, high, body, 0)

    pair = (field, other)
    for repeat in range(SWEEPS):
        sweep(pair[repeat % 2], pair[(repeat + 1) % 2], 1 + repeat, total - 1 - repeat)
    final = pair[SWEEPS % 2]

    def finish(r, c):
        out[r] = final[r + HALO, pl.ds(own, slices), :].T
        return c

    lax.fori_loop(0, rows, finish, 0)
    for copy in copies:
        copy.wait_send()


def smooth(relaxed):
    rows, slices, cols = relaxed.shape
    tall = slices + 24
    return pl.pallas_call(
        sweep_kernel,
        out_shape=jax.ShapeDtypeStruct((rows, cols, slices), F32),
        in_specs=[pl.BlockSpec(memory_space=pltpu.VMEM)],
        out_specs=pl.BlockSpec(memory_space=pltpu.VMEM),
        scratch_shapes=[
            pltpu.VMEM((rows + 2 * HALO, tall, cols), F32),
            pltpu.VMEM((rows + 2 * HALO, tall, cols), F32),
            pltpu.VMEM((tall, cols), F32),
            pltpu.VMEM((tall, cols), F32),
            pltpu.VMEM((4, HALO, slices, cols), BF16),
            pltpu.VMEM((2, rows, 8, cols), F32),
            pltpu.VMEM((2, HALO, 8, cols), F32),
            pltpu.SemaphoreType.DMA((2,)),
            pltpu.SemaphoreType.DMA((2,)),
            pltpu.SemaphoreType.DMA((3,)),
            pltpu.SemaphoreType.DMA((3,)),
        ],
        compiler_params=pltpu.CompilerParams(
            collective_id=1, has_side_effects=True, vmem_limit_bytes=VMEM_LIMIT
        ),
        name="smooth",
    )(relaxed)


def per_device(image, weights, tiles, blocks, owners, count, measured):
    partial = forward(tiles, blocks, owners, count, image, weights)
    residual, spread = exchange(partial, measured)
    relaxed = backward(tiles, blocks, owners, count, image, spread, weights)
    return smooth(relaxed), residual


def solution(mesh):
    placed = (
        P("plane", None, "cuts"),
        P("plane", None, None),
        P("plane"),
        P("plane"),
        P(),
        P("plane"),
        P("plane", None, "cuts"),
    )
    return jax.shard_map(
        per_device,
        mesh=mesh,
        in_specs=placed,
        out_specs=(P("plane", None, "cuts"), P("plane", None, "cuts")),
        check_vma=False,
    )
```

time: 716 us -> 136 us (0.19)
  the two profiles are of different devices: /device:TPU:121 before, /device:TPU:1 now
where the time goes in v1:
time: 136 us
  Pallas kernels  131 us (96%)
  local copies, waits for them, and re-layouts  2.93 us (2%)
    pallas_call x1, Pallas kernels, exchange(): pl.pallas_call(kernel, out_shape=(jax.ShapeDtypeStruct((1, rays, slices),...  65.1 us
    pallas_call x1, Pallas kernels, smooth(): pl.pallas_call(sweep_kernel, out_shape=jax.ShapeDtypeStruct((rows, cols,...  35.8 us
    pallas_call x1, Pallas kernels, backward(): pl.pallas_call(backward_kernel, out_shape=jax.ShapeDtypeStruct((rows, sli...  16 us
    pallas_call x1, Pallas kernels, forward(): pl.pallas_call(forward_kernel, out_shape=jax.ShapeDtypeStruct((slots, 2,...  14.6 us
    unnamed x4, local copies, waits for them, and re-layouts  2.93 us

profile of v1, /device:TPU:1, one launch (start us, length us, event | category | flops | bytes accessed | tf_op | source)
XLA Modules:
  0.0 135.7 jit_solution(1705208461930450733)
XLA Ops:
  1.3 14.6 %project.1 = bf16[64,2,128,128]{3,2,1,0:T(8,128)(2,1)} custom-call(s32[96]{0:T(128)} %tiles.3, s32[96]{0:T(128)} %blocks.3, s32[64]{0:T(128)} %owners.3, s32[1]{0:T(128)S(6)} %copy.11.count, f32[16,128,128]{2,1,0:T(8,128)} %image.3, bf16[96,256,256]{2,1,0:T(8,128)(2,1)} %weights.3), custom_call_target="tpu_custom_call" | custom-call | tf_op jit(solution)/shard_map/project/pallas_call | solution.py:78
  15.9 65.1 %exchange.1 = (bf16[1,256,128]{2,1,0:T(8,128)(2,1)}, bf16[4,4,4,256,128]{4,3,2,1,0:T(8,128)(2,1)}) custom-call(bf16[4,4,4,2,128,128]{5,4,3,2,1,0:T(8,128)(2,1)} %bitcast.2, f32[1,256,128]{2,1,0:T(8,128)} %measured.1), custom_call_target="tpu_custom_call" | custom-call | tf_op jit(solution)/shard_map/exchange/pallas_call | solution.py:334
  81.0 16.0 %backproject.1.relaxed = f32[16,128,128]{2,1,0:T(8,128)} custom-call(s32[96]{0:T(128)} %tiles.3, s32[96]{0:T(128)} %blocks.3, s32[64]{0:T(128)} %owners.3, s32[1]{0:T(128)S(6)} %copy.11.count, f32[16,128,128]{2,1,0:T(8,128)} %image.3, bf16[64,256,128]{2,1,0:T(8,128)(2,1)} %bitcast.3, bf16[96,256,256]{2,1,0:T(8,128)(2,1)} %weights.3), custom_call_target="tpu_custom_call" | custom-call | tf_op jit(solution)/shard_map/backproject/pallas_call | solution.py:131
  97.0 0.0 copy-start
  97.0 35.8 %smooth.1 = f32[16,128,128]{2,1,0:T(8,128)} custom-call(f32[16,128,128]{2,1,0:T(8,128)} %backproject.1.relaxed), custom_call_target="tpu_custom_call" | custom-call | tf_op jit(solution)/shard_map/smooth/pallas_call | solution.py:485
  132.8 2.3 %copy.12 = f32[16,128,128]{2,1,0:T(8,128)} copy(f32[16,128,128]{2,1,0:T(8,128)} %smooth.1) | data formatting | bytes 2097152
  135.1 0.0 copy-done
  135.1 0.6 copy.13
Async XLA Ops:
  97.0 38.1 %copy-start = (bf16[1,256,128]{2,1,0:T(8,128)(2,1)S(1)}, bf16[1,256,128]{2,1,0:T(8,128)(2,1)}, u32[]{:S(2)}) copy-start(bf16[1,256,128]{2,1,0:T(8,128)(2,1)} %get-tuple-element.9) | copy-start | bytes 196612

commit v2 on v1

v2 whole, which is shorter than its diff:
```python
import functools

import jax
import jax.numpy as jnp
from jax import lax
from jax.experimental import pallas as pl
from jax.experimental.pallas import tpu as pltpu
from jax.sharding import PartitionSpec as P

TILE = 16
SWEEPS = 4
smooth_square = 0.09
flow_step = 0.04
relax_step = 4.0

SIDE = 4
HALO = 4
CHUNKS = 4
MIB = 1024 * 1024
ORDERS = ((0, 1, 2), (1, 2, 0), (2, 0, 1))
STREAMS = tuple((i % 3, 16 * i, 16) for i in range(8))

F32 = jnp.float32
BF16 = jnp.bfloat16


def coordinates():
    here = lax.axis_index("plane")
    return here // (SIDE * SIDE), (here // SIDE) % SIDE, here % SIDE


def relative_slot(owner):
    x, y, z = coordinates()
    dx = lax.bitwise_and(owner // (SIDE * SIDE) - x + SIDE, SIDE - 1)
    dy = lax.bitwise_and((owner // SIDE) % SIDE - y + SIDE, SIDE - 1)
    dz = lax.bitwise_and(owner % SIDE - z + SIDE, SIDE - 1)
    return (dx * SIDE + dy) * SIDE + dz


def forward_kernel(*refs):
    tables, (count, image, weights, out, held, rows, voxels, sums, arrived) = refs[:3], refs[3:12]
    tiles, blocks, owners, ready = refs[12:]
    slots = sums.shape[0] - 1
    chunks = arrived.shape[0]
    width = held.shape[0] // chunks

    def load(c):
        part = pl.ds(c * width, width)
        return pltpu.make_async_copy(weights.at[part], held.at[part], arrived.at[c])

    early = [pltpu.make_async_copy(image, rows, ready.at[3])]
    for i, (table, local) in enumerate(zip(tables, refs[12:15])):
        early.append(pltpu.make_async_copy(table, local, ready.at[i]))
    for copy in early:
        copy.start()
    for c in range(chunks):
        load(c).start()

    def clear(i, c):
        sums[i] = jnp.zeros(sums.shape[1:], F32)
        return c

    lax.fori_loop(0, slots, clear, 0)
    for copy in early:
        copy.wait()
    for tile in range(voxels.shape[0]):
        piece = rows[:, tile * TILE : (tile + 1) * TILE, :]
        voxels[tile] = piece.reshape(TILE * TILE, piece.shape[-1]).T.astype(BF16)

    def chunk(c, carry):
        load(c).wait()
        for i in range(width):
            pair = c * width + i
            slot = jnp.where(pair < count[0], relative_slot(owners[blocks[pair]]), slots)
            product = jnp.dot(voxels[tiles[pair]], held[pair], preferred_element_type=F32)
            sums[slot, 0] += product[:, :128]
            sums[slot, 1] += product[:, 128:]
        return carry

    lax.fori_loop(0, chunks, chunk, 0)

    def finish(i, c):
        out[i] = sums[i].astype(BF16)
        return c

    lax.fori_loop(0, slots, finish, 0)


def smem():
    return pl.BlockSpec(memory_space=pltpu.SMEM)


def vmem():
    return pl.BlockSpec(memory_space=pltpu.VMEM)


def forward(*operands):
    owners, _, image, weights = operands[2:]
    pairs, voxels, rays = weights.shape
    rows, cols, slices = image.shape
    slots = owners.shape[0]
    operands = [
        x if i == 3 else pltpu.with_memory_space_constraint(x, pltpu.HBM)
        for i, x in enumerate(operands)
    ]
    hbm = pl.BlockSpec(memory_space=pltpu.HBM)
    return pl.pallas_call(
        forward_kernel,
        out_shape=jax.ShapeDtypeStruct((slots, 2, slices, 128), BF16),
        in_specs=[hbm, hbm, hbm, smem(), hbm, hbm],
        out_specs=vmem(),
        scratch_shapes=[
            pltpu.VMEM((pairs, voxels, rays), BF16),
            pltpu.VMEM((rows, cols, slices), F32),
            pltpu.VMEM((cols // TILE, slices, voxels), BF16),
            pltpu.VMEM((slots + 1, 2, slices, 128), F32),
            pltpu.SemaphoreType.DMA((CHUNKS,)),
            *[pltpu.SMEM(x.shape, jnp.int32) for x in operands[:3]],
            pltpu.SemaphoreType.DMA((4,)),
        ],
        compiler_params=pltpu.CompilerParams(vmem_limit_bytes=30 * MIB),
        name="project",
    )(*operands)


def backward_kernel(tiles, blocks, owners, count, image, spread, weights, out, sums):
    tile_count = sums.shape[0] - 1
    width = weights.shape[0] // CHUNKS
    for i in range(tile_count):
        sums[i] = jnp.zeros(sums.shape[1:], F32)

    def chunk(c, carry):
        for i in range(width):
            pair = c * width + i
            tile = jnp.where(pair < count[0], tiles[pair], tile_count)
            slot = relative_slot(owners[blocks[pair]])
            values = jnp.concatenate([spread[slot, 0], spread[slot, 1]], axis=1)
            sums[tile] += lax.dot_general(
                values, weights[pair], (((1,), (1,)), ((), ())), preferred_element_type=F32
            )
        return carry

    lax.fori_loop(0, CHUNKS, chunk, 0)
    rows, cols, slices = image.shape
    for tile in range(tile_count):
        here = slice(tile * TILE, (tile + 1) * TILE)
        update = sums[tile].T.reshape(rows, TILE, slices)
        out[:, here, :] = jnp.maximum(image[:, here, :] + relax_step * update, 0.0)


def backward(tiles, blocks, owners, count, image, spread, weights):
    pairs, voxels, rays = weights.shape
    rows, cols, slices = image.shape
    return pl.pallas_call(
        backward_kernel,
        out_shape=jax.ShapeDtypeStruct((rows, cols, slices), F32),
        in_specs=[smem(), smem(), smem(), smem(), vmem(), vmem(), vmem()],
        out_specs=vmem(),
        scratch_shapes=[pltpu.VMEM((cols // TILE + 1, slices, voxels), F32)],
        compiler_params=pltpu.CompilerParams(vmem_limit_bytes=24 * MIB),
        name="backproject",
    )(tiles, blocks, owners, count, image, spread, weights)


def neighbour(dim, shift):
    place = list(coordinates())
    place[dim] = (place[dim] + shift + SIDE) % SIDE
    return (place[0] * SIDE + place[1]) * SIDE + place[2]


def pick(order, *where):
    index = [slice(None)] * 3
    for position, value in enumerate(where):
        index[ORDERS[order][position]] = value
    return tuple(index)


def exchange_kernel(partial, measured, residual, gather, wanted, own, buffers, sems):
    sum_send, sum_recv, spread_send, spread_recv = sems

    barrier = pltpu.get_barrier_semaphore()
    for dim in range(3):
        for shift in (1, 2, 3):
            pl.semaphore_signal(barrier, inc=1, device_id={"plane": neighbour(dim, shift)})
    for half in range(2):
        wanted[half] = measured[0, half * 128 : (half + 1) * 128, :].T
    pl.semaphore_wait(barrier, 9)
    sends = []

    def combine(target, first, *others):
        def one(index):
            value = first[index].astype(F32)
            for other in others:
                value = value + other[index].astype(F32)
            target[index] = value.astype(target.dtype)

        blocks = target.shape[:-2]
        if len(blocks) == 2:

            def body(i, c):
                for k in range(blocks[1]):
                    one((i, k))
                return c

            lax.fori_loop(0, blocks[0], body, 0)
        elif len(blocks) == 1:
            for k in range(blocks[0]):
                one((k,))
        else:
            one((slice(None),))

    def stages(number):
        order, first, rows = STREAMS[number]
        part_rows = pl.ds(first, rows)
        opposite, direct, nearest, late, middle, total = buffers[number]

        def source(phase, j, half):
            if phase == 0:
                return partial.at[pick(order, j) + (half, part_rows)]
            return middle.at[pick(order, 0, j) + (half,)]

        def send(pool, slot, phase, src, dst, shift):
            copy = pltpu.make_async_remote_copy(
                src_ref=src,
                dst_ref=dst,
                send_sem=pool[0].at[number, slot],
                recv_sem=pool[1].at[number, slot],
                device_id={"plane": neighbour(ORDERS[order][phase], shift)},
            )
            copy.start()
            sends.append(copy)
            return copy

        adding = (sum_send, sum_recv)
        spreading = (spread_send, spread_recv)
        state = {}

        def sum_early(phase):
            opp, dirs = opposite[phase], direct[phase]
            state["opp"] = [
                send(adding, 6 * phase, phase, source(phase, 2, 0), opp.at[0], 1),
                send(adding, 6 * phase + 1, phase, source(phase, 2, 1), opp.at[1], -1),
            ]
            state["dir"] = [
                send(adding, 6 * phase + 2, phase, source(phase, 1, 1), dirs.at[0, 1], 1),
                send(adding, 6 * phase + 3, phase, source(phase, 3, 0), dirs.at[1, 0], -1),
            ]

        def sum_late(phase):
            opp, dirs = opposite[phase], direct[phase]
            for half, (j, shift) in enumerate(((1, 1), (3, -1))):
                state["opp"][half].wait_recv()
                here = source(phase, j, half)
                joined = late.at[half] if phase == 0 else here
                combine(joined, here, opp.at[half])
                state["dir"].append(
                    send(adding, 6 * phase + 4 + half, phase, joined, dirs.at[half, half], shift)
                )

        def sum_end(phase):
            dirs = direct[phase]
            for copy in state["dir"]:
                copy.wait_recv()
            for half in range(2):
                if phase == 0:
                    target = middle.at[pick(order, 0) + (half,)]
                else:
                    target = total.at[:, half]
                combine(target, source(phase, 0, half), dirs.at[0, half], dirs.at[1, half])

        def sum_nearest():
            state["near"] = [
                send(adding, 11 + j, 2, total.at[j], nearest.at[j - 1], j) for j in (2, 1, 3)
            ]

        def settle():
            for copy in state["near"]:
                copy.wait_recv()
            for half in range(2):
                reached = total[0, half]
                for i in range(3):
                    reached = reached + nearest[i, half]
                mismatch = wanted[half, part_rows] - reached
                value = (mismatch * lax.rsqrt(1.0 + mismatch * mismatch)).astype(BF16)
                own[half, part_rows] = value.astype(F32)
                gather[0, 0, 0, half, part_rows] = value

        def held(phase, j, *half):
            index = pick(order, *([0] * phase), j)
            return gather.at[index + ((half[0] if half else slice(None)), part_rows)]

        def spread_nearest():
            state["near"] = [
                send(spreading, 7 + j, 2, held(2, 0), held(2, SIDE - j), j) for j in (2, 1, 3)
            ]

        def spread_met():
            for copy in state["near"]:
                copy.wait_recv()

        def spread_early(phase):
            slot = 4 * phase
            state["one"] = [
                send(spreading, slot, phase, held(phase, 0), held(phase, 3), 1),
                send(spreading, slot + 1, phase, held(phase, 0), held(phase, 1), -1),
            ]

        def spread_late(phase):
            slot = 4 * phase + 2
            state["two"] = []
            for half, (j, shift) in enumerate(((3, 1), (1, -1))):
                state["one"][half].wait_recv()
                state["two"].append(
                    send(spreading, slot + half, phase, held(phase, j, half), held(phase, 2, half), shift)
                )

        def spread_end(phase):
            for copy in state["two"]:
                copy.wait_recv()

        def together(*steps):
            def run():
                for step, *args in steps:
                    step(*args)

            return run

        return [
            together((sum_early, 0)),
            together((sum_late, 0)),
            together((sum_end, 0), (sum_early, 1)),
            together((sum_late, 1)),
            together((sum_end, 1), (sum_nearest,)),
            together((settle,), (spread_nearest,)),
            together((spread_met,), (spread_early, 1)),
            together((spread_late, 1)),
            together((spread_end, 1), (spread_early, 0)),
            together((spread_late, 0)),
            together((spread_end, 0)),
        ]

    plan = []
    for number in range(len(STREAMS)):
        for k, run in enumerate(stages(number)):
            plan.append((k, number, run))
    plan.sort(key=lambda entry: entry[:2])
    for _, _, run in plan:
        run()

    for half in range(2):
        residual[0, half * 128 : (half + 1) * 128, :] = own[half].T.astype(BF16)
    for copy in sends:
        copy.wait_send()


def exchange(partial, measured):
    slots, halves, slices, lanes = partial.shape
    rays = measured.shape[1]
    cube = (SIDE, SIDE, SIDE)
    count = len(STREAMS)
    buffers = []
    for order, _, rows in STREAMS:
        for blocks in ((SIDE, SIDE), (SIDE,)):
            buffers.append(pltpu.VMEM((2, *blocks, rows, lanes), BF16))
        for blocks in ((SIDE, SIDE), (SIDE,)):
            buffers.append(pltpu.VMEM((2, 2, *blocks, rows, lanes), BF16))
        thin = [1 if dim == ORDERS[order][0] else SIDE for dim in range(3)]
        buffers.append(pltpu.VMEM((3, halves, rows, lanes), F32))
        buffers.append(pltpu.VMEM((2, SIDE, SIDE, rows, lanes), BF16))
        buffers.append(pltpu.VMEM((*thin, halves, rows, lanes), BF16))
        buffers.append(pltpu.VMEM((SIDE, halves, rows, lanes), F32))
    each = len(buffers) // count

    def kernel(partial, measured, residual, gather, wanted, own, *rest):
        grouped = []
        for i in range(count):
            mine = rest[each * i : each * (i + 1)]
            grouped.append((mine[0:2], mine[2:4], *mine[4:]))
        exchange_kernel(
            partial, measured, residual, gather, wanted, own, grouped, rest[each * count :]
        )

    residual, spread = pl.pallas_call(
        kernel,
        out_shape=(
            jax.ShapeDtypeStruct((1, rays, slices), BF16),
            jax.ShapeDtypeStruct((*cube, halves, slices, lanes), BF16),
        ),
        in_specs=[vmem(), vmem()],
        out_specs=(vmem(), vmem()),
        scratch_shapes=[
            pltpu.VMEM((halves, slices, lanes), F32),
            pltpu.VMEM((halves, slices, lanes), F32),
            *buffers,
            pltpu.SemaphoreType.DMA((count, 15)),
            pltpu.SemaphoreType.DMA((count, 15)),
            pltpu.SemaphoreType.DMA((count, 11)),
            pltpu.SemaphoreType.DMA((count, 11)),
        ],
        compiler_params=pltpu.CompilerParams(
            collective_id=0, has_side_effects=True, vmem_limit_bytes=24 * MIB
        ),
        name="exchange",
    )(partial.reshape(*cube, halves, slices, lanes), measured)
    return residual, spread.reshape(slots, halves, slices, lanes)


def sweep_kernel(image, out, relaxed, field, other, flux_rows, flux_slices, edge, side, corner, *sems):
    row_send, row_recv, side_send, side_recv = sems
    rows, slices, cols = relaxed.shape
    here = lax.axis_index("plane")
    cut = lax.axis_index("cuts")
    last = lax.axis_size("plane") - 1
    up = (here + last) % (last + 1)
    down = (here + 1) % (last + 1)
    base = 8 + 8 * cut

    def turn(r, c):
        relaxed[r] = image[r].T
        return c

    barrier = pltpu.get_barrier_semaphore()
    for plane in (up, down):
        for core in (0, 1):
            pl.semaphore_signal(barrier, inc=1, device_id={"plane": plane, "cuts": core})
    pl.semaphore_signal(barrier, inc=1, device_id={"plane": here, "cuts": 1 - cut})
    lax.fori_loop(0, rows, turn, 0)
    pl.semaphore_wait(barrier, 5)

    edge[0] = relaxed[rows - HALO :].astype(BF16)
    edge[1] = relaxed[:HALO].astype(BF16)
    start = pl.multiple_of(120 * (1 - cut), 8)
    side[0] = relaxed[:, pl.ds(start, 8), :]
    copies = []

    def send(src, dst, plane, core, number, which):
        copy = pltpu.make_async_remote_copy(
            src_ref=src,
            dst_ref=dst,
            send_sem=which[0].at[number],
            recv_sem=which[1].at[number],
            device_id={"plane": plane, "cuts": core},
        )
        copy.start()
        copies.append(copy)

    send(side.at[0], side.at[1], here, 1 - cut, 0, (side_send, side_recv))
    send(side.at[0, pl.ds(rows - HALO, HALO)], corner.at[0], down, 1 - cut, 1, (side_send, side_recv))
    send(side.at[0, pl.ds(0, HALO)], corner.at[1], up, 1 - cut, 2, (side_send, side_recv))
    send(edge.at[0], edge.at[2], down, cut, 0, (row_send, row_recv))
    send(edge.at[1], edge.at[3], up, cut, 1, (row_send, row_recv))

    total = rows + 2 * HALO
    zero = jnp.zeros((8, cols), F32)
    chunks = (slices + 8) // 8

    def clear(i, c):
        for array in (field, other):
            array[i, pl.ds(0, 8), :] = zero
            array[i, pl.ds(slices + 16, 8), :] = zero
        return c

    lax.fori_loop(0, total, clear, 0)
    for i in range(2):
        flux_slices[i, pl.ds(0, 8), :] = zero
    own = pl.multiple_of(base, 8)
    beyond = pl.multiple_of(8 + slices * (1 - cut), 8)
    field[pl.ds(HALO, rows), pl.ds(own, slices), :] = relaxed[...]
    copies[0].wait_recv()
    field[pl.ds(HALO, rows), pl.ds(beyond, 8), :] = side[1]

    lane = lax.broadcasted_iota(jnp.int32, (8, cols), 1)
    not_last = lane < cols - 1
    not_first = lane > 0
    first_row = here * rows - HALO
    row_limit = (last + 1) * rows

    def sweep(old, new, low, high, edge_rows):
        def weight(r):
            if not edge_rows:
                return flow_step
            inside = jnp.logical_and(first_row + r >= 0, first_row + r < row_limit)
            return jnp.where(inside, flow_step, 0.0)

        def flux(r, at, value, below, step):
            rise_rows = below - value
            rise_slices = old[r, at + 1 : at + 9, :] - value
            rise_cols = jnp.where(not_last, pltpu.roll(value, cols - 1, 1), 0.0) - value
            square = rise_rows * rise_rows + rise_cols * rise_cols + rise_slices * rise_slices
            scale = lax.rsqrt(smooth_square + square) * step
            return rise_rows * scale, rise_cols * scale, rise_slices * scale

        step = weight(low - 1)
        for chunk in range(chunks):
            at = 8 + 8 * chunk
            value = old[low - 1, at : at + 8, :]
            flux_rows[at : at + 8, :] = flux(low - 1, at, value, old[low, at : at + 8, :], step)[0]

        def body(i, c):
            r = low + 2 * i
            steps = (weight(r), weight(r + 1))
            for chunk in range(chunks):
                at = 8 + 8 * chunk
                here_rows = [old[r + k, at : at + 8, :] for k in range(3)]
                passed = flux_rows[at : at + 8, :]
                for k in range(2):
                    value = here_rows[k]
                    along_rows, along_cols, along_slices = flux(
                        r + k, at, value, here_rows[k + 1], steps[k]
                    )
                    flux_slices[k, at : at + 8, :] = along_slices
                    before = jnp.where(not_first, pltpu.roll(along_cols, 1, 1), 0.0)
                    diverge = (along_rows - passed) + (along_cols - before)
                    diverge = diverge + (along_slices - flux_slices[k, at - 1 : at + 7, :])
                    new[r + k, at : at + 8, :] = value + diverge
                    passed = along_rows
                flux_rows[at : at + 8, :] = passed
            return c

        lax.fori_loop(0, (high - low) // 2, body, 0)

    pair = (field, other)
    for repeat in range(SWEEPS):
        old, new = pair[repeat % 2], pair[(repeat + 1) % 2]
        sweep(old, new, HALO + 1 + repeat, HALO + rows - 1 - repeat, False)

    above = (here > 0).astype(F32)
    below = (here < last).astype(F32)
    for copy in copies[1:]:
        copy.wait_recv()
    field[pl.ds(0, HALO), pl.ds(own, slices), :] = edge[2].astype(F32) * above
    field[pl.ds(0, HALO), pl.ds(beyond, 8), :] = corner[0] * above
    field[pl.ds(HALO + rows, HALO), pl.ds(own, slices), :] = edge[3].astype(F32) * below
    field[pl.ds(HALO + rows, HALO), pl.ds(beyond, 8), :] = corner[1] * below
    for repeat in range(SWEEPS):
        old, new = pair[repeat % 2], pair[(repeat + 1) % 2]
        sweep(old, new, 1 + repeat, HALO + 1 + repeat, True)
        sweep(old, new, HALO + rows - 1 - repeat, 2 * HALO + rows - 1 - repeat, True)
        if repeat < SWEEPS - 1:
            new[HALO + rows] = new[HALO + rows] * below
    final = pair[SWEEPS % 2]

    def finish(r, c):
        out[r] = final[r + HALO, pl.ds(own, slices), :].T
        return c

    lax.fori_loop(0, rows, finish, 0)
    for copy in copies:
        copy.wait_send()


def smooth(relaxed):
    rows, cols, slices = relaxed.shape
    tall = slices + 24
    return pl.pallas_call(
        sweep_kernel,
        out_shape=jax.ShapeDtypeStruct((rows, cols, slices), F32),
        in_specs=[pl.BlockSpec(memory_space=pltpu.VMEM)],
        out_specs=pl.BlockSpec(memory_space=pltpu.VMEM),
        scratch_shapes=[
            pltpu.VMEM((rows, slices, cols), F32),
            pltpu.VMEM((rows + 2 * HALO, tall, cols), F32),
            pltpu.VMEM((rows + 2 * HALO, tall, cols), F32),
            pltpu.VMEM((tall, cols), F32),
            pltpu.VMEM((2, tall, cols), F32),
            pltpu.VMEM((4, HALO, slices, cols), BF16),
            pltpu.VMEM((2, rows, 8, cols), F32),
            pltpu.VMEM((2, HALO, 8, cols), F32),
            pltpu.SemaphoreType.DMA((2,)),
            pltpu.SemaphoreType.DMA((2,)),
            pltpu.SemaphoreType.DMA((3,)),
            pltpu.SemaphoreType.DMA((3,)),
        ],
        compiler_params=pltpu.CompilerParams(
            collective_id=1, has_side_effects=True, vmem_limit_bytes=20 * MIB
        ),
        name="smooth",
    )(relaxed)


def per_device(image, weights, tiles, blocks, owners, count, measured):
    partial = forward(tiles, blocks, owners, count, image, weights)
    partial, weights = lax.optimization_barrier((partial, weights))
    residual, spread = exchange(partial, measured)
    relaxed = backward(tiles, blocks, owners, count, image, spread, weights)
    return smooth(relaxed), residual


def solution(mesh):
    placed = (
        P("plane", None, "cuts"),
        P("plane", None, None),
        P("plane"),
        P("plane"),
        P(),
        P("plane"),
        P("plane", None, "cuts"),
    )
    return jax.shard_map(
        per_device,
        mesh=mesh,
        in_specs=placed,
        out_specs=(P("plane", None, "cuts"), P("plane", None, "cuts")),
        check_vma=False,
    )
```

time: 136 us -> 90.2 us (0.66)
  Pallas kernels: 131 us -> 87 us
    pallas_call x1, Pallas kernels: 65.1 us -> 51.7 us  [exchange(): pl.pallas_call(kernel, out_shape=(jax.ShapeDtypeStruct((1, rays, slices),...]
    pallas_call x1, Pallas kernels: 35.8 us -> 23.1 us  [smooth(): pl.pallas_call(sweep_kernel, out_shape=jax.ShapeDtypeStruct((rows, cols,...]
    pallas_call x1, Pallas kernels: 16 us -> 5.61 us  [backward(): pl.pallas_call(backward_kernel, out_shape=jax.ShapeDtypeStruct((rows, col...]
    pallas_call x1, Pallas kernels: 14.6 us -> 6.57 us  [forward(): pl.pallas_call(forward_kernel, out_shape=jax.ShapeDtypeStruct((slots, 2,...]
    unnamed x4 -> x14, local copies, waits for them, and re-layouts: 2.93 us -> 1.64 us
where the time goes in v2:
time: 90.2 us; the launch traced here: 90 us
  Pallas kernels  87 us (96%)
  local copies, waits for them, and re-layouts  1.64 us (2%)
  between operations  1.4 us (2%)
    pallas_call x1, Pallas kernels, exchange(): pl.pallas_call(kernel, out_shape=(jax.ShapeDtypeStruct((1, rays, slices),...  51.7 us
    pallas_call x1, Pallas kernels, smooth(): pl.pallas_call(sweep_kernel, out_shape=jax.ShapeDtypeStruct((rows, cols,...  23.1 us
    pallas_call x1, Pallas kernels, forward(): pl.pallas_call(forward_kernel, out_shape=jax.ShapeDtypeStruct((slots, 2,...  6.57 us
    pallas_call x1, Pallas kernels, backward(): pl.pallas_call(backward_kernel, out_shape=jax.ShapeDtypeStruct((rows, col...  5.61 us

profile of v2, /device:TPU:1, one launch (start us, length us, event | category | flops | bytes accessed | tf_op | source)
XLA Modules:
  0.0 90.0 jit_solution(3326446947962907743)
XLA Ops:
  1.3 0.0 copy-start.2
  1.3 0.0 copy-start
  1.3 6.6 %project.1 = bf16[64,2,128,128]{3,2,1,0:T(8,128)(2,1)S(1)} custom-call(s32[96]{0:T(128)} %tiles.1, s32[96]{0:T(128)} %blocks.1, s32[64]{0:T(128)} %owners.1, s32[1]{0:T(128)S(6)} %copy.11.refs_3_.count, f32[16,128,128]{2,1,0:T(8,128)} %image.1, bf16[96,256,256]{2,1,0:T(8,128)(2,1)} %weights), custom_call_target="tpu_custom_call" | custom-call | tf_op jit(solution)/shard_map/project/pallas_call | solution.py:107
  7.9 0.0 copy-start.1
  7.9 0.0 copy-start.3
  7.9 0.0 copy-start.4
  7.9 0.0 copy-start.5
  7.9 0.0 copy-done.2
  7.9 51.7 %exchange.1 = (bf16[1,256,128]{2,1,0:T(8,128)(2,1)S(1)}, bf16[4,4,4,2,128,128]{5,4,3,2,1,0:T(8,128)(2,1)S(1)}) custom-call(bf16[4,4,4,2,128,128]{5,4,3,2,1,0:T(8,128)(2,1)S(1)} %bitcast.2, f32[1,256,128]{2,1,0:T(8,128)S(1)} %copy-done.2), custom_call_target="tpu_custom_call" | custom-call | tf_op jit(solution)/shard_map/exchange/pallas_call | solution.py:383
  59.7 0.0 copy-done
  59.7 0.0 copy-done.1
  59.7 0.0 copy-done.3
  59.7 0.0 copy-done.4
  59.7 0.0 copy-done.5
  59.7 5.6 %backproject.1.image = f32[16,128,128]{2,1,0:T(8,128)S(1)} custom-call(s32[96]{0:T(128)S(1)} %copy-done.3, s32[96]{0:T(128)S(1)} %copy-done.4, s32[64]{0:T(128)S(1)} %copy-done.5, s32[1]{0:T(128)S(6)} %copy.11.refs_3_.count, f32[16,128,128]{2,1,0:T(8,128)S(1)} %copy-done.1, bf16[64,2,128,128]{3,2,1,0:T(8,128)(2,1)S(1)} %bitcast.3, ...), custom_call_target="tpu_custom_call" | custom-call | tf_op jit(solution)/shard_map/backproject/pallas_call | solution.py:154
  65.3 23.1 %smooth.1 = f32[16,128,128]{2,1,0:T(8,128)S(1)} custom-call(f32[16,128,128]{2,1,0:T(8,128)S(1)} %backproject.1.image), custom_call_target="tpu_custom_call" | custom-call | tf_op jit(solution)/shard_map/smooth/pallas_call | solution.py:555
  88.4 1.0 %copy.12 = f32[16,128,128]{2,1,0:T(8,128)} copy(f32[16,128,128]{2,1,0:T(8,128)S(1)} %smooth.1) | data formatting | bytes 2097152
  89.4 0.6 copy.13
Async XLA Ops:
  1.3 6.7 %copy-start.2 = (f32[1,256,128]{2,1,0:T(8,128)S(1)}, f32[1,256,128]{2,1,0:T(8,128)}, u32[]{:S(2)}) copy-start(f32[1,256,128]{2,1,0:T(8,128)} %measured.1) | copy-start | bytes 393220
  1.3 58.4 %copy-start = (bf16[96,256,256]{2,1,0:T(8,128)(2,1)S(1)}, bf16[96,256,256]{2,1,0:T(8,128)(2,1)}, u32[]{:S(2)}) copy-start(bf16[96,256,256]{2,1,0:T(8,128)(2,1)} %weights) | copy-start | bytes 37748740
  7.9 51.8 %copy-start.1 = (f32[16,128,128]{2,1,0:T(8,128)S(1)}, f32[16,128,128]{2,1,0:T(8,128)}, u32[]{:S(2)}) copy-start(f32[16,128,128]{2,1,0:T(8,128)} %image.1) | copy-start | bytes 3145732
  7.9 51.8 %copy-start.3 = (s32[96]{0:T(128)S(1)}, s32[96]{0:T(128)}, u32[]{:S(2)}) copy-start(s32[96]{0:T(128)} %tiles.1) | copy-start | bytes 1156
  7.9 51.8 %copy-start.4 = (s32[96]{0:T(128)S(1)}, s32[96]{0:T(128)}, u32[]{:S(2)}) copy-start(s32[96]{0:T(128)} %blocks.1) | copy-start | bytes 1156
  7.9 51.8 %copy-start.5 = (s32[64]{0:T(128)S(1)}, s32[64]{0:T(128)}, u32[]{:S(2)}) copy-start(s32[64]{0:T(128)} %owners.1) | copy-start | bytes 772
